TPU v7x, 512 devices: a whole 4x4x16 slice. The times are simulated.
512 devices in a mesh: row: 16 (over z_lo, core), col: 16 (over y, x), gz: 2 (over z_hi).
Axes of the slice: x: 4, y: 4, z: 16 (z_hi: 2, z_lo: 8; z = z_hi * 8 + z_lo), core: 2. Of those that a mesh axis runs over, the one named last changes fastest.
Arguments:
- modes: bfloat16 [64, 96, 32, 3, 2048], P('row', 'col', 'gz'), may hold values from -0.109375 to 0.109375
- blocks: float32 [8, 7, 3, 3], replicated, may hold values from -6 to 6
- material: int32 [64, 96, 32], P('row', 'col', 'gz'), may hold values from 0 to 7
Outputs:
- reduced: float32 [2048, 256], P('col')
All inputs are finite; a program needn't handle non-finite values.
Results may differ from a plain program's by a relative error of at most 0.0029.
Values may be sent and summed in bfloat16 or wider, within the bound.
No kernel may reach another device: no remote copies, remote signals or barrier semaphores. Data moves between devices by JAX's collectives and lax.ppermute only.
A program may use at most 64 MiB of HBM per device.

v0:
```python
import jax
import jax.numpy as jnp
from jax import lax
from jax.sharding import PartitionSpec as P

PANEL = 256
NMAT = 8


def with_halo(value, sides, width):
    for axis, dim in sides:
        devices, length = (lax.axis_size(axis), value.shape[dim])
        up = [(i, (i + 1) % devices) for i in range(devices - 1)]
        down = [(j, i) for i, j in up]
        last = lax.slice_in_dim(value, length - width, length, axis=dim)
        first = lax.slice_in_dim(value, 0, width, axis=dim)
        before = lax.ppermute(last, axis, up)
        after = lax.ppermute(first, axis, down)
        value = jnp.concatenate([before, value, after], axis=dim)
    return value


def couplings(material, blocks):
    kinds = jnp.arange(NMAT, dtype=jnp.int32)
    onehot = (material[..., None] == kinds).astype(jnp.float32)
    table = blocks.reshape(NMAT, 63)
    flat = jnp.einsum("xyzm,mk->xyzk", onehot, table, precision=lax.Precision.HIGHEST)
    return flat.reshape(material.shape + (7, 3, 3))


def neighbours(padded):
    centre = padded[1:-1, 1:-1, 1:-1]
    return [
        centre,
        padded[2:, 1:-1, 1:-1],
        padded[:-2, 1:-1, 1:-1],
        padded[1:-1, 2:, 1:-1],
        padded[1:-1, :-2, 1:-1],
        padded[1:-1, 1:-1, 2:],
        padded[1:-1, 1:-1, :-2],
    ]


def apply_blocks(padded, coupling):
    pieces = neighbours(padded)
    result = jnp.zeros(pieces[0].shape, jnp.float32)
    for offset in range(7):
        result = result + jnp.einsum(
            "xyzij,xyzjc->xyzic",
            coupling[:, :, :, offset],
            pieces[offset],
            precision=lax.Precision.HIGHEST,
        )
    return result


def shards(modes, blocks, material):
    panel = modes[..., :PANEL]
    padded = with_halo(panel, (("row", 0), ("col", 1), ("gz", 2)), 1)
    coupling = couplings(material, blocks)
    stiff_panel = apply_blocks(padded.astype(jnp.float32), coupling).astype(jnp.bfloat16)
    flat_modes = modes.reshape(-1, modes.shape[-1])
    flat_stiff = stiff_panel.reshape(-1, PANEL)
    tile_rows = lax.psum_scatter(
        lax.dot_general(
            flat_modes, flat_stiff, (((0,), (0,)), ((), ())), preferred_element_type=jnp.float32
        ),
        "col",
        scatter_dimension=0,
        tiled=True,
    )
    shared = lax.psum_scatter(tile_rows, "row", scatter_dimension=0, tiled=True)
    summed = lax.psum(shared, "gz")
    reduced = lax.all_gather(summed, "row", axis=0, tiled=True)
    return reduced


def solution(mesh):
    return jax.shard_map(
        shards,
        mesh=mesh,
        in_specs=(P("row", "col", "gz", None, None), P(), P("row", "col", "gz")),
        out_specs=P("col", None),
        check_vma=False,
    )
```

profile of v0, /device:TPU:1, one launch (start us, length us, event | category | flops | bytes accessed | tf_op | source)
XLA Modules:
  0.0 332.2 jit_solution(4879748920144390912)
XLA Ops:
  8.3 4.9 %collective-permute-start.1 = (bf16[1,6,16,3,256]{4,3,2,1,0:T(4,128)(2,1)}, bf16[1,6,16,3,256]{4,3,2,1,0:T(4,128)(2,1)S(1)}, u32[]{:S(2)}, u32[]{:S(2)}) collective-permute-start(bf16[1,6,16,3,256]{4,3,2,1,0:T(4,128)(2,1)} %copy.59), channel_id=1, source_target_pairs={{0,32},{32,64},{64,96},{96,128},{128,160},{160,192},{192,224},{224... | collective-permute-start | bytes 442376 | tf_op jit(solution)/shard_map/ppermute | solution.py:17
  14.0 5.1 %collective-permute-start = (bf16[1,6,16,3,256]{4,3,2,1,0:T(4,128)(2,1)}, bf16[1,6,16,3,256]{4,3,2,1,0:T(4,128)(2,1)S(1)}, u32[]{:S(2)}, u32[]{:S(2)}) collective-permute-start(bf16[1,6,16,3,256]{4,3,2,1,0:T(4,128)(2,1)} %copy.58), channel_id=1, source_target_pairs={{32,0},{64,32},{96,64},{128,96},{160,128},{192,160},{224,192},{256... | collective-permute-start | bytes 442376 | tf_op jit(solution)/shard_map/ppermute | solution.py:18
  22.9 1.6 fusion.18
  24.4 1.4 copy.54
  25.8 2.3 copy.53
  28.1 2.3 copy.52
  30.4 2.3 copy.51
  32.7 2.3 copy.50
  34.9 1.4 copy.49
  40.0 1.6 fusion.10
  41.6 1.6 fusion.8
  43.2 3.9 %collective-permute-done.2 = bf16[6,1,16,3,256]{4,3,2,1,0:T(4,128)(2,1)S(1)} collective-permute-done((bf16[6,1,16,3,256]{4,3,2,1,0:T(4,128)(2,1)S(1)}, bf16[6,1,16,3,256]{4,3,2,1,0:T(4,128)(2,1)S(1)}, u32[]{:S(2)}, u32[]{:S(2)}) %collective-permute-start.2) | collective-permute-done | bytes 147488 | tf_op jit(solution)/shard_map/ppermute | solution.py:18
  47.4 1.4 collective-permute-start.4
  48.8 12.9 %collective-permute-start.5 = (bf16[6,8,1,3,256]{4,1,3,2,0:T(8,128)(2,1)S(1)}, bf16[6,8,1,3,256]{4,1,3,2,0:T(8,128)(2,1)S(1)}, u32[]{:S(2)}, u32[]{:S(2)}) collective-permute-start(bf16[6,8,1,3,256]{4,1,3,2,0:T(8,128)(2,1)S(1)} %copy.38), channel_id=1, source_target_pairs={{0,1},{2,3},{4,5},{6,7},{8,9},{10,11},{12,13},{14,15},{16,17},{18,... | collective-permute-start | bytes 221192 | tf_op jit(solution)/shard_map/ppermute | solution.py:17
  61.7 1.6 fusion.6
  63.3 1.6 fusion.4
  66.1 1.6 fusion.2
  67.7 3.3 add_convert_fusion
  71.0 2.9 convolution_bitcast_fusion
  74.0 93.6 %reduce-scatter.5.cloned.1.call-done = f32[128,256]{0,1:T(8,128)} async-done(((f32[2048,256]{0,1:T(8,128)}), f32[128,256]{0,1:T(8,128)}) %reduce-scatter.5.cloned.1.call-update) | async-done | bytes 131088 | tf_op jit(solution)/shard_map/reduce_scatter | solution.py:64
  167.6 1.7 copy.55
  169.3 99.0 %reduce-scatter.7.cloned.1.call-done = f32[8,256]{1,0:T(8,128)} async-done(((f32[128,256]{1,0:T(8,128)}), f32[8,256]{1,0:T(8,128)}) %reduce-scatter.7.cloned.1.call-update) | async-done | bytes 8208
  269.1 24.8 %psum.7 = f32[8,256]{0,1:T(8,128)S(1)} all-reduce(f32[8,256]{0,1:T(8,128)S(1)} %copy.56), channel_id=1, replica_groups=mesh['row'=16,'col'=16,'gz'=2] {'gz'}, use_global_device_ids=true, to_apply=%region_2.0 | all-reduce | flops 2048 | bytes 16384 | tf_op jit(solution)/shard_map/psum | solution.py:73
  294.0 30.7 %all_gather.3 = f32[128,256]{1,0:T(8,128)S(1)} all-gather(f32[8,256]{1,0:T(8,128)S(1)} %copy.42), channel_id=1, replica_groups=mesh['row'=16,'col'=16,'gz'=2] {'row'}, dimensions={0}, use_global_device_ids=true | all-gather | bytes 139264 | tf_op jit(solution)/shard_map/all_gather | solution.py:74
  (53 shorter events, 12.7 us)
Async XLA Ops:
  6.5 13.8 %copy-start.6 = (s32[4,6,16]{2,0,1:T(4,128)S(1)}, s32[4,6,16]{2,0,1:T(4,128)}, u32[]{:S(2)}) copy-start(s32[4,6,16]{2,0,1:T(4,128)} %param.5) | copy-start | bytes 4612
  6.5 13.8 %copy-start.5 = (f32[8,7,3,3]{1,0,3,2:T(8,128)S(1)}, f32[8,7,3,3]{1,0,3,2:T(8,128)}, u32[]{:S(2)}) copy-start(f32[8,7,3,3]{1,0,3,2:T(8,128)} %param.4) | copy-start | bytes 6052
  6.5 161.1 %reduce-scatter.5.cloned.1.call-start = ((), (), s32[]{:S(2)}) async-start(), calls=%async_computation.2 | async-start | bytes 2228224 | tf_op jit(solution)/shard_map/reduce_scatter | solution.py:64
  8.3 28.0 %collective-permute-start.1 = (bf16[1,6,16,3,256]{4,3,2,1,0:T(4,128)(2,1)}, bf16[1,6,16,3,256]{4,3,2,1,0:T(4,128)(2,1)S(1)}, u32[]{:S(2)}, u32[]{:S(2)}) collective-permute-start(bf16[1,6,16,3,256]{4,3,2,1,0:T(4,128)(2,1)} %copy.59), channel_id=1, source_target_pairs={{0,32},{32,64},{64,96},{96,128},{128,160},{160,192},{192,224},{224... | collective-permute-start | bytes 442376 | tf_op jit(solution)/shard_map/ppermute | solution.py:17
  14.0 23.0 %collective-permute-start = (bf16[1,6,16,3,256]{4,3,2,1,0:T(4,128)(2,1)}, bf16[1,6,16,3,256]{4,3,2,1,0:T(4,128)(2,1)S(1)}, u32[]{:S(2)}, u32[]{:S(2)}) collective-permute-start(bf16[1,6,16,3,256]{4,3,2,1,0:T(4,128)(2,1)} %copy.58), channel_id=1, source_target_pairs={{32,0},{64,32},{96,64},{128,96},{160,128},{192,160},{224,192},{256... | collective-permute-start | bytes 442376 | tf_op jit(solution)/shard_map/ppermute | solution.py:18
  36.4 3.6 %copy-start.3 = (f32[4,6,16,1,3,3]{5,4,2,1,0,3:T(4,128)S(1)}, f32[4,6,16,1,3,3]{5,4,2,1,0,3:T(4,128)}, u32[]{:S(2)}) copy-start(f32[4,6,16,1,3,3]{5,4,2,1,0,3:T(4,128)} %copy.49) | copy-start | bytes 41476
  37.4 5.9 %collective-permute-start.3 = (bf16[6,1,16,3,256]{4,3,2,1,0:T(4,128)(2,1)S(1)}, bf16[6,1,16,3,256]{4,3,2,1,0:T(4,128)(2,1)S(1)}, u32[]{:S(2)}, u32[]{:S(2)}) collective-permute-start(bf16[6,1,16,3,256]{4,3,2,1,0:T(4,128)(2,1)S(1)} %get-tuple-element.9), channel_id=1, source_target_pairs={{0,2},{2,4},{4,6},{6,8},{8,10},{10,12},{12,14},{14,16},{16,18},{18... | collective-permute-start | bytes 442376 | tf_op jit(solution)/shard_map/ppermute | solution.py:17
  38.7 8.5 %collective-permute-start.2 = (bf16[6,1,16,3,256]{4,3,2,1,0:T(4,128)(2,1)S(1)}, bf16[6,1,16,3,256]{4,3,2,1,0:T(4,128)(2,1)S(1)}, u32[]{:S(2)}, u32[]{:S(2)}) collective-permute-start(bf16[6,1,16,3,256]{4,3,2,1,0:T(4,128)(2,1)S(1)} %get-tuple-element.10), channel_id=1, source_target_pairs={{2,0},{4,2},{6,4},{8,6},{10,8},{12,10},{14,12},{16,14},{18,16},{20... | collective-permute-start | bytes 442376 | tf_op jit(solution)/shard_map/ppermute | solution.py:18
  40.0 1.6 copy-start.2
  43.2 18.5 %copy-start.1 = (f32[4,6,16,1,3,3]{5,4,2,1,0,3:T(4,128)S(1)}, f32[4,6,16,1,3,3]{5,4,2,1,0,3:T(4,128)}, u32[]{:S(2)}) copy-start(f32[4,6,16,1,3,3]{5,4,2,1,0,3:T(4,128)} %copy.51) | copy-start | bytes 41476
  47.3 16.0 %copy-start = (f32[4,6,16,1,3,3]{5,4,2,1,0,3:T(4,128)S(1)}, f32[4,6,16,1,3,3]{5,4,2,1,0,3:T(4,128)}, u32[]{:S(2)}) copy-start(f32[4,6,16,1,3,3]{5,4,2,1,0,3:T(4,128)} %copy.52) | copy-start | bytes 41476
  47.4 17.6 %collective-permute-start.4 = (bf16[6,8,1,3,256]{4,1,3,2,0:T(8,128)(2,1)S(1)}, bf16[6,8,1,3,256]{4,1,3,2,0:T(8,128)(2,1)S(1)}, u32[]{:S(2)}, u32[]{:S(2)}) collective-permute-start(bf16[6,8,1,3,256]{4,1,3,2,0:T(8,128)(2,1)S(1)} %copy.34), channel_id=1, source_target_pairs={{1,0},{3,2},{5,4},{7,6},{9,8},{11,10},{13,12},{15,14},{17,16},{19,... | collective-permute-start | bytes 221192 | tf_op jit(solution)/shard_map/ppermute | solution.py:18
  48.8 17.2 %collective-permute-start.5 = (bf16[6,8,1,3,256]{4,1,3,2,0:T(8,128)(2,1)S(1)}, bf16[6,8,1,3,256]{4,1,3,2,0:T(8,128)(2,1)S(1)}, u32[]{:S(2)}, u32[]{:S(2)}) collective-permute-start(bf16[6,8,1,3,256]{4,1,3,2,0:T(8,128)(2,1)S(1)} %copy.38), channel_id=1, source_target_pairs={{0,1},{2,3},{4,5},{6,7},{8,9},{10,11},{12,13},{14,15},{16,17},{18,... | collective-permute-start | bytes 221192 | tf_op jit(solution)/shard_map/ppermute | solution.py:17
  63.3 2.7 copy-start.4
  66.1 5.0 %slice-start = ((s8[4718592]{0:T(1024)(128)(4,1)}), s8[4194304]{0:T(1024)(128)(4,1)S(1)}, s32[]{:S(2)}) async-start(s8[4718592]{0:T(1024)(128)(4,1)} %bitcast.45), calls=%async_computation.4 | async-start | bytes 8388608
  67.7 3.3 %slice-start.1 = ((s8[4718592]{0:T(1024)(128)(4,1)}), s8[524288]{0:T(1024)(128)(4,1)S(1)}, s32[]{:S(2)}) async-start(s8[4718592]{0:T(1024)(128)(4,1)} %bitcast.45), calls=%async_computation.5 | async-start | bytes 1048576
  74.0 194.4 %reduce-scatter.7.cloned.1.call-start = ((), (), s32[]{:S(2)}) async-start(), calls=%async_computation.3 | async-start | bytes 139264
Sparse Core Ops, SparseCore 0:
  74.1 93.4 reduce-scatter.4
  170.6 97.6 reduce-scatter.6
where the time goes:
time: 333 us; the launch traced here: 332 us
  waiting for transfers between devices  198 us (59%)
  blocking collectives  55.5 us (17%)
  starting transfers between devices  27 us (8%)
  local copies, waits for them, and re-layouts  21.9 us (7%)
  matrix products  16.3 us (5%)
  between operations  13.8 us (4%)
    unnamed x3, waiting for transfers between devices  99.1 us
    reduce_scatter x1, waiting for transfers between devices, shards(): lax.psum_scatter(lax.dot_general(flat_modes, flat_stiff, (((0,), (0,)), (...  93.6 us
    all_gather x1, blocking collectives, shards(): reduced = lax.all_gather(summed, 'row', axis=0, tiled=True)  30.7 us
    psum x1, blocking collectives, shards(): summed = lax.psum(shared, 'gz')  24.8 us
    ppermute x3, starting transfers between devices, with_halo(): before = lax.ppermute(last, axis, up)  19.1 us
    dot_general x7, matrix products, apply_blocks(): jnp.einsum('xyzij,xyzjc->xyzic', coupling[:, :, :, offset], pieces[offset...  12.9 us
    squeeze x7, local copies, waits for them, and re-layouts, apply_blocks(): coupling[:, :, :, offset]  12.4 us
    ppermute x3, starting transfers between devices, with_halo(): after = lax.ppermute(first, axis, down)  7.86 us
  transfers between devices with their start and end apart: 8, of which 4 were waited for; matrix products, arithmetic and copies ran while one was open for 8% of the time, Pallas kernels for 0%

commit v1 on v0

--- a/solution.py
+++ b/solution.py
@@ -70,7 +70,7 @@
         tiled=True,
     )
     shared = lax.psum_scatter(tile_rows, "row", scatter_dimension=0, tiled=True)
-    summed = lax.psum(shared, "gz")
+    summed = jnp.sum(lax.all_gather(shared, "gz"), axis=0)
     reduced = lax.all_gather(summed, "row", axis=0, tiled=True)
     return reduced
 

time: 333 us -> 321 us (0.964)
  blocking collectives: 55.5 us -> 46.7 us
    reduce_scatter x0 -> x1, waiting for transfers between devices: none -> 99.1 us  [shards(): shared = lax.psum_scatter(tile_rows, 'row', scatter_dimension=0, tiled=True)]
    unnamed x3 -> x2, waiting for transfers between devices: 99.1 us -> 0.03 us
    psum x1 -> x0, blocking collectives: 24.8 us -> none  [shards(): summed = lax.psum(shared, 'gz')]
    all_gather x0 -> x1, blocking collectives: none -> 12.1 us  [shards(): summed = jnp.sum(lax.all_gather(shared, 'gz'), axis=0)]
    all_gather x1, blocking collectives: 30.7 us -> 34.6 us  [shards(): reduced = lax.all_gather(summed, 'row', axis=0, tiled=True)]
  transfers between devices with their start and end apart: 8 -> 8, of which waited for: 4 -> 4; matrix products, arithmetic and copies ran while one was open for 8% -> 7% of each run, Pallas kernels for 0% -> 0%
where the time goes in v1:
time: 321 us
  waiting for transfers between devices  197 us (61%)
  blocking collectives  46.7 us (15%)
  starting transfers between devices  27 us (8%)
  local copies, waits for them, and re-layouts  19.3 us (6%)
  matrix products  17.2 us (5%)
  between operations  13.8 us (4%)
    reduce_scatter x1, waiting for transfers between devices, shards(): shared = lax.psum_scatter(tile_rows, 'row', scatter_dimension=0, tiled=True)  99.1 us
    reduce_scatter x1, waiting for transfers between devices, shards(): lax.psum_scatter(lax.dot_general(flat_modes, flat_stiff, (((0,), (0,)), (...  93.6 us
    all_gather x1, blocking collectives, shards(): reduced = lax.all_gather(summed, 'row', axis=0, tiled=True)  34.6 us
    ppermute x3, starting transfers between devices, with_halo(): before = lax.ppermute(last, axis, up)  19.1 us
    dot_general x7, matrix products, apply_blocks(): jnp.einsum('xyzij,xyzjc->xyzic', coupling[:, :, :, offset], pieces[offset...  13.9 us
    all_gather x1, blocking collectives, shards(): summed = jnp.sum(lax.all_gather(shared, 'gz'), axis=0)  12.1 us
    squeeze x7, local copies, waits for them, and re-layouts, apply_blocks(): coupling[:, :, :, offset]  9.76 us
    ppermute x3, starting transfers between devices, with_halo(): after = lax.ppermute(first, axis, down)  7.86 us
  transfers between devices with their start and end apart: 8, of which 4 were waited for; matrix products, arithmetic and copies ran while one was open for 7% of the time, Pallas kernels for 0%

profile of v1, /device:TPU:1, one launch (start us, length us, event | category | flops | bytes accessed | tf_op | source)
XLA Modules:
  0.0 320.9 jit_solution(611665845469267598)
XLA Ops:
  8.3 4.9 %collective-permute-start.1 = (bf16[1,6,16,3,256]{4,3,2,1,0:T(4,128)(2,1)}, bf16[1,6,16,3,256]{4,3,2,1,0:T(4,128)(2,1)S(1)}, u32[]{:S(2)}, u32[]{:S(2)}) collective-permute-start(bf16[1,6,16,3,256]{4,3,2,1,0:T(4,128)(2,1)} %copy.58), channel_id=1, source_target_pairs={{0,32},{32,64},{64,96},{96,128},{128,160},{160,192},{192,224},{224... | collective-permute-start | bytes 442376 | tf_op jit(solution)/shard_map/ppermute | solution.py:17
  14.1 5.1 %collective-permute-start = (bf16[1,6,16,3,256]{4,3,2,1,0:T(4,128)(2,1)}, bf16[1,6,16,3,256]{4,3,2,1,0:T(4,128)(2,1)}, u32[]{:S(2)}, u32[]{:S(2)}) collective-permute-start(bf16[1,6,16,3,256]{4,3,2,1,0:T(4,128)(2,1)} %copy.57), channel_id=1, source_target_pairs={{32,0},{64,32},{96,64},{128,96},{160,128},{192,160},{224,192},{256... | collective-permute-start | bytes 442376 | tf_op jit(solution)/shard_map/ppermute | solution.py:18
  22.9 1.6 fusion.18
  24.5 2.3 copy.53
  26.8 1.4 copy.52
  28.2 1.4 copy.51
  29.6 1.4 copy.50
  31.0 1.4 copy.49
  32.3 1.4 copy.48
  38.3 2.6 fusion.10
  40.9 1.6 fusion.8
  42.5 2.9 collective-permute-done.2
  45.6 1.4 collective-permute-start.4
  47.1 12.9 %collective-permute-start.5 = (bf16[6,8,1,3,256]{4,1,3,2,0:T(8,128)(2,1)S(1)}, bf16[6,8,1,3,256]{4,1,3,2,0:T(8,128)(2,1)S(1)}, u32[]{:S(2)}, u32[]{:S(2)}) collective-permute-start(bf16[6,8,1,3,256]{4,1,3,2,0:T(8,128)(2,1)S(1)} %copy.37), channel_id=1, source_target_pairs={{0,1},{2,3},{4,5},{6,7},{8,9},{10,11},{12,13},{14,15},{16,17},{18,... | collective-permute-start | bytes 221192 | tf_op jit(solution)/shard_map/ppermute | solution.py:17
  60.0 1.6 fusion.6
  61.6 1.6 fusion.4
  64.4 1.6 fusion.2
  66.0 3.3 %add_convert_fusion = bf16[4,6,16,3,256]{4,3,2,1,0:T(4,128)(2,1)S(1)} fusion(f32[4,6,16,3,256]{4,3,2,1,0:T(4,128)S(1)} %fusion.2, f32[4,6,16,3,256]{4,3,2,1,0:T(4,128)S(1)} %fusion.4, f32[4,6,16,3,256]{4,3,2,1,0:T(4,128)S(1)} %fusion.6, f32[4,6,16,3,256]{4,3,2,1,0:T(4,128)S(1)} %fusion.8, f32[4,6,16,3,256]{4,3,2,1,0:T(4,128)S(1)} %fusion.18, ...), kind=kOutput, calls=%fused_computation.1 | convolution fusion | flops 15040512 | bytes 8934912 | tf_op jit(solution)/shard_map/xyzij,xyzjc->xyzic/dot_general | solution.py:48
  69.4 2.9 convolution_bitcast_fusion
  72.3 93.6 %reduce-scatter.5.cloned.1.call-done = f32[128,256]{0,1:T(8,128)} async-done(((f32[2048,256]{0,1:T(8,128)}), f32[128,256]{0,1:T(8,128)}) %reduce-scatter.5.cloned.1.call-update) | async-done | bytes 131088 | tf_op jit(solution)/shard_map/reduce_scatter | solution.py:64
  165.9 1.7 copy.54
  167.6 99.1 %reduce-scatter.7.cloned.1.call-done = f32[8,256]{1,0:T(8,128)} async-done(((f32[128,256]{1,0:T(8,128)}), f32[8,256]{1,0:T(8,128)}) %reduce-scatter.7.cloned.1.call-update) | async-done | bytes 8208 | tf_op jit(solution)/shard_map/reduce_scatter | solution.py:72
  266.6 12.1 %all-gather = f32[16,256]{1,0:T(8,128)S(1)} all-gather(f32[8,256]{1,0:T(8,128)} %reduce-scatter.7.cloned.1.call-done), channel_id=2, replica_groups=mesh['row'=16,'col'=16,'gz'=2] {'gz'}, dimensions={0}, use_global_device_ids=true | all-gather | bytes 24576 | tf_op jit(solution)/shard_map/all_gather | solution.py:73
  278.8 34.6 %all_gather.11 = f32[128,256]{1,0:T(8,128)S(1)} all-gather(f32[8,256]{1,0:T(8,128)S(1)} %bitcast_reduce_fusion), channel_id=1, replica_groups=mesh['row'=16,'col'=16,'gz'=2] {'row'}, dimensions={0}, use_global_device_ids=true | all-gather | bytes 139264 | tf_op jit(solution)/shard_map/all_gather | solution.py:74
  (60 shorter events, 12.7 us)
Async XLA Ops:
  6.5 13.8 %copy-start.10 = (s32[4,6,16]{2,0,1:T(4,128)S(1)}, s32[4,6,16]{2,0,1:T(4,128)}, u32[]{:S(2)}) copy-start(s32[4,6,16]{2,0,1:T(4,128)} %param.5) | copy-start | bytes 4612
  6.5 13.8 %copy-start.9 = (f32[8,7,3,3]{1,0,3,2:T(8,128)S(1)}, f32[8,7,3,3]{1,0,3,2:T(8,128)}, u32[]{:S(2)}) copy-start(f32[8,7,3,3]{1,0,3,2:T(8,128)} %param.4) | copy-start | bytes 6052
  6.5 159.4 %reduce-scatter.5.cloned.1.call-start = ((), (), s32[]{:S(2)}) async-start(), calls=%async_computation.2 | async-start | bytes 2228224 | tf_op jit(solution)/shard_map/reduce_scatter | solution.py:64
  8.3 25.4 %collective-permute-start.1 = (bf16[1,6,16,3,256]{4,3,2,1,0:T(4,128)(2,1)}, bf16[1,6,16,3,256]{4,3,2,1,0:T(4,128)(2,1)S(1)}, u32[]{:S(2)}, u32[]{:S(2)}) collective-permute-start(bf16[1,6,16,3,256]{4,3,2,1,0:T(4,128)(2,1)} %copy.58), channel_id=1, source_target_pairs={{0,32},{32,64},{64,96},{96,128},{128,160},{160,192},{192,224},{224... | collective-permute-start | bytes 442376 | tf_op jit(solution)/shard_map/ppermute | solution.py:17
  14.1 20.4 %collective-permute-start = (bf16[1,6,16,3,256]{4,3,2,1,0:T(4,128)(2,1)}, bf16[1,6,16,3,256]{4,3,2,1,0:T(4,128)(2,1)}, u32[]{:S(2)}, u32[]{:S(2)}) collective-permute-start(bf16[1,6,16,3,256]{4,3,2,1,0:T(4,128)(2,1)} %copy.57), channel_id=1, source_target_pairs={{32,0},{64,32},{96,64},{128,96},{160,128},{192,160},{224,192},{256... | collective-permute-start | bytes 442376 | tf_op jit(solution)/shard_map/ppermute | solution.py:18
  22.9 3.9 %copy-start.8 = (f32[4,6,16,1,3,3]{2,3,5,4,1,0:T(1,128)S(1)}, f32[4,6,16,1,3,3]{2,3,5,4,1,0:T(1,128)}, u32[]{:S(2)}) copy-start(f32[4,6,16,1,3,3]{2,3,5,4,1,0:T(1,128)} %get-tuple-element.12) | copy-start | bytes 41476
  24.4 3.8 %copy-start.7 = (f32[4,6,16,1,3,3]{2,3,5,4,1,0:T(1,128)S(1)}, f32[4,6,16,1,3,3]{2,3,5,4,1,0:T(1,128)}, u32[]{:S(2)}) copy-start(f32[4,6,16,1,3,3]{2,3,5,4,1,0:T(1,128)} %get-tuple-element.13) | copy-start | bytes 41476
  24.5 5.1 %copy-start.6 = (f32[4,6,16,1,3,3]{2,3,5,4,1,0:T(1,128)S(1)}, f32[4,6,16,1,3,3]{2,3,5,4,1,0:T(1,128)}, u32[]{:S(2)}) copy-start(f32[4,6,16,1,3,3]{2,3,5,4,1,0:T(1,128)} %get-tuple-element.14) | copy-start | bytes 41476
  33.8 4.5 %copy-start.4 = (f32[4,6,16,1,3,3]{5,4,2,1,0,3:T(4,128)S(1)}, f32[4,6,16,1,3,3]{5,4,2,1,0,3:T(4,128)}, u32[]{:S(2)}) copy-start(f32[4,6,16,1,3,3]{5,4,2,1,0,3:T(4,128)} %copy.48) | copy-start | bytes 41476
  35.7 6.9 %collective-permute-start.3 = (bf16[6,1,16,3,256]{4,3,2,1,0:T(4,128)(2,1)S(1)}, bf16[6,1,16,3,256]{4,3,2,1,0:T(4,128)(2,1)S(1)}, u32[]{:S(2)}, u32[]{:S(2)}) collective-permute-start(bf16[6,1,16,3,256]{4,3,2,1,0:T(4,128)(2,1)S(1)} %get-tuple-element.9), channel_id=1, source_target_pairs={{0,2},{2,4},{4,6},{6,8},{8,10},{10,12},{12,14},{14,16},{16,18},{18... | collective-permute-start | bytes 442376 | tf_op jit(solution)/shard_map/ppermute | solution.py:17
  37.0 8.5 %collective-permute-start.2 = (bf16[6,1,16,3,256]{4,3,2,1,0:T(4,128)(2,1)S(1)}, bf16[6,1,16,3,256]{4,3,2,1,0:T(4,128)(2,1)S(1)}, u32[]{:S(2)}, u32[]{:S(2)}) collective-permute-start(bf16[6,1,16,3,256]{4,3,2,1,0:T(4,128)(2,1)S(1)} %get-tuple-element.10), channel_id=1, source_target_pairs={{2,0},{4,2},{6,4},{8,6},{10,8},{12,10},{14,12},{16,14},{18,16},{20... | collective-permute-start | bytes 442376 | tf_op jit(solution)/shard_map/ppermute | solution.py:18
  38.3 2.6 copy-start.3
  42.5 17.5 %copy-start.2 = (f32[4,6,16,1,3,3]{5,4,2,1,0,3:T(4,128)S(1)}, f32[4,6,16,1,3,3]{5,4,2,1,0,3:T(4,128)}, u32[]{:S(2)}) copy-start(f32[4,6,16,1,3,3]{5,4,2,1,0,3:T(4,128)} %copy.50) | copy-start | bytes 41476
  45.6 16.0 %copy-start.1 = (f32[4,6,16,1,3,3]{5,4,2,1,0,3:T(4,128)S(1)}, f32[4,6,16,1,3,3]{5,4,2,1,0,3:T(4,128)}, u32[]{:S(2)}) copy-start(f32[4,6,16,1,3,3]{5,4,2,1,0,3:T(4,128)} %copy.51) | copy-start | bytes 41476
  45.6 17.6 %collective-permute-start.4 = (bf16[6,8,1,3,256]{4,1,3,2,0:T(8,128)(2,1)S(1)}, bf16[6,8,1,3,256]{4,1,3,2,0:T(8,128)(2,1)S(1)}, u32[]{:S(2)}, u32[]{:S(2)}) collective-permute-start(bf16[6,8,1,3,256]{4,1,3,2,0:T(8,128)(2,1)S(1)} %copy.33), channel_id=1, source_target_pairs={{1,0},{3,2},{5,4},{7,6},{9,8},{11,10},{13,12},{15,14},{17,16},{19,... | collective-permute-start | bytes 221192 | tf_op jit(solution)/shard_map/ppermute | solution.py:18
  47.1 17.2 %collective-permute-start.5 = (bf16[6,8,1,3,256]{4,1,3,2,0:T(8,128)(2,1)S(1)}, bf16[6,8,1,3,256]{4,1,3,2,0:T(8,128)(2,1)S(1)}, u32[]{:S(2)}, u32[]{:S(2)}) collective-permute-start(bf16[6,8,1,3,256]{4,1,3,2,0:T(8,128)(2,1)S(1)} %copy.37), channel_id=1, source_target_pairs={{0,1},{2,3},{4,5},{6,7},{8,9},{10,11},{12,13},{14,15},{16,17},{18,... | collective-permute-start | bytes 221192 | tf_op jit(solution)/shard_map/ppermute | solution.py:17
  61.6 2.7 copy-start.5
  64.3 1.6 copy-start
  64.4 5.0 %slice-start = ((s8[4718592]{0:T(1024)(128)(4,1)}), s8[4194304]{0:T(1024)(128)(4,1)S(1)}, s32[]{:S(2)}) async-start(s8[4718592]{0:T(1024)(128)(4,1)} %bitcast.47), calls=%async_computation.4 | async-start | bytes 8388608
  66.0 3.3 %slice-start.1 = ((s8[4718592]{0:T(1024)(128)(4,1)}), s8[524288]{0:T(1024)(128)(4,1)S(1)}, s32[]{:S(2)}) async-start(s8[4718592]{0:T(1024)(128)(4,1)} %bitcast.47), calls=%async_computation.5 | async-start | bytes 1048576
  72.2 194.4 %reduce-scatter.7.cloned.1.call-start = ((), (), s32[]{:S(2)}) async-start(), calls=%async_computation.3 | async-start | bytes 139264 | tf_op jit(solution)/shard_map/reduce_scatter | solution.py:72
Sparse Core Ops, SparseCore 0:
  72.4 93.4 reduce-scatter.4
  168.9 97.6 reduce-scatter.6
